TPU v7x, 128 devices: a whole 4x4x4 slice. The times are simulated.
128 devices in a mesh: expert: 8 (over y, core), tok: 16 (over z, x).
Axes of the slice: x: 4, y: 4, z: 4, core: 2. Of those that a mesh axis runs over, the one named last changes fastest.
Arguments:
- hidden: bfloat16 [8, 4096, 2048], P('expert', 'tok'), may hold values from -40 to 40, as said below
- token_ids: int32 [8, 4096], P('expert', 'tok'), may hold values from 0 to 128004, as said below
- weights: bfloat16 [8, 2048, 8192], P('expert', None, 'tok'), may hold values from -6 to 6
Outputs:
- merged: float32 [2048, 8192], P(None, 'tok')
Inputs may be any that keep to these rules, and one draw needn't show every extreme that they name: `token_ids`: each expert's tokens come in sequences of 128 slots: slot 0 holds 128000, then between 63 and 126 further token ids below 128000, then the padding id 128004 in the remaining slots (one or more). `hidden`: channel scales differ by up to a factor of ten.
All inputs are finite; a program needn't handle non-finite values.
Results may differ from a plain program's by a relative error of at most 0.0017.
Values may be sent and summed in bfloat16 or wider, within the bound.
A program may use at most 256 MiB of HBM per device.

v0:
```python
import functools

import jax
import jax.numpy as jnp
from jax import lax
from jax.experimental import pallas as pl
from jax.experimental.pallas import tpu as pltpu
from jax.sharding import PartitionSpec as P

F32, BF16 = jnp.float32, jnp.bfloat16
MESH = pl.DeviceIdType.MESH
SIDE = 4
INNER_TOL = 4e-3
OUTER_TOL = 2e-5
ROWS = 16


def near(i, step):
    return (i + step + SIDE) % SIDE


def remote(sems, index, source, target, device):
    send, recv = sems
    return pltpu.make_async_remote_copy(
        src_ref=source, dst_ref=target, send_sem=send.at[index], recv_sem=recv.at[index],
        device_id=device, device_id_type=MESH,
    )


def meet(devices):
    barrier = pltpu.get_barrier_semaphore()
    for device in devices:
        pl.semaphore_signal(barrier, inc=1, device_id=device, device_id_type=MESH)
    pl.semaphore_wait(barrier, len(devices))


def build_kernel(toks, x_hbm, ids_ref, w_ref, s, b_ref, X, cat, acc, wt, stat, stats, gr, pg, hg, rg, sg, pt, ht, far, close,
                 send, recv, own, stat_send, stat_recv):
    e, t = lax.axis_index("expert"), lax.axis_index("tok")
    y, c = e // 2, e % 2
    z, x = t // SIDE, t % SIDE
    width, cols = w_ref.shape
    band = width // toks
    half = x_hbm.shape[0] // 2
    count = iter(range(send.shape[0]))

    def rc(source, target, device):
        return remote((send, recv), next(count), source, target, device)

    def tok(zz, xx):
        return {"tok": zz * SIDE + xx}

    def chip(yy):
        return {"expert": yy * 2 + c}

    partner = {"expert": e + 1 - 2 * c}
    up, down, across = near(y, 1), near(y, -1), near(y, 2)
    meet([{"tok": (t + k) % toks} for k in range(1, toks)] + [partner, chip(up), chip(down), chip(across)])
    mine = (X.at[z, x], X.at[SIDE + x, z])
    loads = [pltpu.make_async_copy(x_hbm.at[pl.ds(k * half, half)], mine[k], own.at[k]) for k in range(2)]
    for load in loads:
        load.start()

    def stage(block, part, to, here):
        above, below = near(here, 1), near(here, -1)
        first = [rc(block(here), block(here), to(above)), rc(block(here), block(here), to(below))]
        onward = [rc(part(below, 0), part(below, 0), to(above)), rc(part(above, 1), part(above, 1), to(below))]
        return first, onward

    quarter = half // 2
    a_first, a_onward = stage(
        lambda i: X.at[z, i], lambda i, h: X.at[z, i, pl.ds(h * quarter, quarter)], lambda i: tok(z, i), x)
    b_first, b_onward = stage(
        lambda i: X.at[SIDE + x, i], lambda i, h: X.at[SIDE + x, i, pl.ds(h * quarter, quarter)], lambda i: tok(i, x), z)

    loads[0].wait()
    for copy in a_first:
        copy.start()
    loads[1].wait()
    for copy in b_first:
        copy.start()

    def clear(i, k):
        at = pl.ds(pl.multiple_of(i * ROWS, ROWS), ROWS)
        acc[at, :] = jnp.zeros((ROWS, width), F32)
        return k

    lax.fori_loop(0, acc.shape[0] // ROWS, clear, 0)

    live = jnp.sum(jnp.where(ids_ref[...] != 128004, 1.0, 0.0), axis=(0, 1), keepdims=True)

    def square(i, total):
        at = pl.ds(pl.multiple_of(i * ROWS, ROWS), ROWS)
        a = X[z, x, at, :].astype(F32)
        b = X[SIDE + x, z, at, :].astype(F32)
        return total + jnp.sum(a * a + b * b, axis=0, keepdims=True)

    stat[:, :width] = lax.fori_loop(0, half // ROWS, square, jnp.zeros((1, width), F32))
    stat[:, width:] = jnp.broadcast_to(live, (1, 128))

    def turn(i, k):
        at = pl.ds(pl.multiple_of(i * 256, 256), 256)
        wt[:, at] = w_ref[at, :].T
        return k

    lax.fori_loop(0, width // 256, turn, 0)

    for got, copy in zip(a_first + b_first, a_onward + b_onward):
        got.wait_recv()
        copy.start()

    def share(k):
        return pltpu.make_async_remote_copy(
            src_ref=stat, dst_ref=stats.at[k], send_sem=stat_send.at[k], recv_sem=stat_recv.at[k],
            device_id={"tok": (t + k) % toks}, device_id_type=MESH,
        )

    for copy in a_onward + b_onward:
        copy.wait_recv()

    def group(g_of, to, here):
        above, below = near(here, 1), near(here, -1)
        first, onward = [], []
        for h in range(2):
            part = X.at[g_of(here), pl.ds(2 * h, 2)]
            first.append([rc(part, part, to(above)), rc(part, part, to(below))])
            lower, upper = X.at[g_of(below), 2 * h], X.at[g_of(above), 2 * h + 1]
            onward.append([rc(lower, lower, to(above)), rc(upper, upper, to(below))])
        return first, onward

    a_near, a_far = group(lambda i: i, lambda i: tok(i, x), z)
    b_near, b_far = group(lambda i: SIDE + i, lambda i: tok(z, i), x)
    for h in range(2):
        for copy in a_near[h] + b_near[h]:
            copy.start()

    lax.fori_loop(1, toks, lambda k, v: (share(k).start(), v)[1], 0)

    pair = 2 * half

    def blocks(kind, off, h):
        here = z * (1 - kind) + x * kind
        return X.at[kind * SIDE + (here + off) % SIDE, pl.ds(2 * h, 2)]

    def put_up(block):
        rows = block[...].reshape(pair, width)
        cat[:cols, :] = jnp.dot(rows, w_ref[...], preferred_element_type=F32).astype(BF16).T

    def put_own(block):
        cat[cols:, :] = block[:, :, pl.ds(pl.multiple_of(t * band, band), band)].reshape(pair, band).T

    def add(block, low, high):
        def tile(n, k):
            at = pl.ds(pl.multiple_of(n * 512, 512), 512)
            acc[low:high, at] += jnp.dot(cat[low:high, :], block[:, :, at].reshape(pair, 512), preferred_element_type=F32)
            return k

        lax.fori_loop(0, width // 512, tile, 0)

    def both(block):
        put_up(block)
        put_own(block)
        add(block, 0, cols + band)

    def step(i, k):
        for h in range(2):
            @pl.when(i == 4 + 4 * h)
            def _(h=h):
                for got, copy in zip(a_near[h] + b_near[h], a_far[h] + b_far[h]):
                    got.wait_recv()
                    copy.start()

        q, m = i // 4, i % 4
        a = m % 2
        close_by = (q + 1) // 2
        both(blocks(m // 2, close_by * (3 - 2 * a), (1 - close_by) * a + close_by * (q // 2)))
        return k

    lax.fori_loop(0, 12, step, 0)

    def last(i, k):
        for kind, copies in enumerate((a_far[0], b_far[0])):
            @pl.when(i == kind)
            def _(copies=copies):
                for copy in copies:
                    copy.wait_recv()

        both(blocks(i, 2, 0))
        return k

    lax.fori_loop(0, 2, last, 0)

    lax.fori_loop(1, toks, lambda k, v: (share(k).wait_recv(), v)[1], 0)
    total = stat[...]
    for k in range(1, toks):
        total = total + stats[k]
    inverse = 1.0 / total[:, width : width + 1]
    squares = total[:, :width] * (0.1 * inverse)

    for kind, copies in enumerate((a_far[1], b_far[1])):
        for copy in copies:
            copy.wait_recv()
        put_own(blocks(kind, 2, 1))
        add(blocks(kind, 2, 1), cols, cols + band)

    def pack(i, k):
        at = pl.ds(pl.multiple_of(cols + i * ROWS, ROWS), ROWS)
        for o in range(toks // 2 + 1):
            block = pl.ds(pl.multiple_of((t + o) % toks * band, band), band)
            gr[i // 4, i % 4, :, o * band : (o + 1) * band] = acc[at, block] * inverse
        return k

    lax.fori_loop(0, band // ROWS, pack, 0)

    swap_g = rc(gr.at[1 - c], pg, partner)
    swap_g.start()

    def finish_up(kind):
        put_up(blocks(kind, 2, 1))
        add(blocks(kind, 2, 1), 0, cols)

    finish_up(0)

    swap_g.wait_recv()
    for k in range(4):
        hg[k] = gr[c, k] + pg[k]
    scatter = [rc(hg.at[near(y, k)], rg.at[k - 1], chip(near(y, k))) for k in range(1, 4)]
    for copy in scatter:
        copy.start()

    finish_up(1)

    for copy in scatter:
        copy.wait_recv()
    sg[...] = hg[y] + rg[0] + rg[1] + rg[2]
    rows = s.at[z, x, c, y // 2, pl.ds((y % 2) * ROWS, ROWS)]
    keep = pltpu.make_async_copy(sg, rows, own.at[0])
    keep.start()
    spread_g = [rc(sg, rows, chip(near(y, k))) for k in range(1, 4)]
    for copy in spread_g:
        copy.start()

    share_rows = cols // 8

    def rows_of(yy, cc):
        return pl.ds(pl.multiple_of(yy * 2 * share_rows + cc * share_rows, share_rows), share_rows)

    def finish(cc):
        def tile(i, k):
            per = share_rows // ROWS
            at = pl.ds(pl.multiple_of(i // per * 2 * share_rows + cc * share_rows + i % per * ROWS, ROWS), ROWS)
            acc[at, :] = acc[at, :] * (0.9 * inverse) + squares * wt[at, :].astype(F32)
            return k

        lax.fori_loop(0, 4 * share_rows // ROWS, tile, 0)

    finish(1 - c)
    swap_t = [rc(acc.at[rows_of(k, 1 - c)], pt.at[k], partner) for k in range(4)]
    for copy in swap_t:
        copy.start()

    keep.wait()
    for copy in spread_g:
        copy.wait_recv()

    a_first_g, a_onward_g = stage(lambda i: s.at[z, i, c, 0], lambda i, h: s.at[z, i, c, 0, pl.ds(16 * h, 16)], lambda i: tok(z, i), x)
    b_first_g, b_onward_g = stage(lambda i: s.at[i, x, c, 1], lambda i, h: s.at[i, x, c, 1, pl.ds(16 * h, 16)], lambda i: tok(i, x), z)
    for copy in a_first_g + b_first_g:
        copy.start()

    finish(c)

    for k in range(4):
        swap_t[k].wait_recv()
        ht[k] = acc[rows_of(k, c), :] + pt[k]
    mid = share_rows // 2
    first_t = [
        rc(ht.at[across, pl.ds(0, mid)], far.at[0], chip(up)),
        rc(ht.at[across, pl.ds(mid, mid)], far.at[1], chip(down)),
    ]
    for copy in first_t:
        copy.start()

    for got, copy in zip(a_first_g + b_first_g, a_onward_g + b_onward_g):
        got.wait_recv()
        copy.start()
    for copy in a_onward_g + b_onward_g:
        copy.wait_recv()

    a_near_g, a_far_g = stage(lambda i: s.at[i, :, c, 0], lambda i, h: s.at[i, pl.ds(2 * h, 2), c, 0], lambda i: tok(i, x), z)
    b_near_g, b_far_g = stage(lambda i: s.at[:, i, c, 1], lambda i, h: s.at[pl.ds(2 * h, 2), i, c, 1], lambda i: tok(z, i), x)
    for copy in a_near_g + b_near_g:
        copy.start()

    def hand(block):
        copy = rc(block, block, partner)
        copy.start()
        return copy

    hands = [hand(s.at[z, :, c, 0]), hand(s.at[:, x, c, 1])]

    first_t[0].wait_recv()
    ht[up, :mid] = ht[up, :mid] + far[0]
    first_t[1].wait_recv()
    ht[down, mid:] = ht[down, mid:] + far[1]
    second_t = [rc(ht.at[up], close.at[0], chip(up)), rc(ht.at[down], close.at[1], chip(down))]
    for copy in second_t:
        copy.start()

    for got, copy in zip(a_near_g + b_near_g, a_far_g + b_far_g):
        got.wait_recv()
        copy.start()
    hands += [hand(s.at[near(z, -1), :, c, 0]), hand(s.at[near(z, 1), :, c, 0])]
    hands += [hand(s.at[:, near(x, -1), c, 1]), hand(s.at[:, near(x, 1), c, 1])]

    for copy in second_t:
        copy.wait_recv()
    b_ref[...] = ht[y] + close[0] + close[1]

    for copy in a_far_g + b_far_g:
        copy.wait_recv()
    hands += [hand(s.at[near(z, 2), :, c, 0]), hand(s.at[:, near(x, 2), c, 1])]
    for copy in hands:
        copy.wait_recv()

    sent = a_first + b_first + a_onward + b_onward
    for h in range(2):
        sent += a_near[h] + b_near[h] + a_far[h] + b_far[h]
    sent += [swap_g] + scatter + spread_g + swap_t + first_t + second_t
    sent += a_first_g + b_first_g + a_onward_g + b_onward_g + a_near_g + b_near_g + a_far_g + b_far_g + hands
    for copy in sent:
        copy.wait_send()
    lax.fori_loop(1, toks, lambda k, v: (share(k).wait_send(), v)[1], 0)


def build(masked, ids, weight, toks):
    count, width = masked.shape
    cols = weight.shape[1]
    band = width // toks
    half = count // 2
    keep = (toks // 2 + 1) * band
    part, share = band // 8, cols // 8
    copies = 67
    vmem = pl.BlockSpec(memory_space=pltpu.VMEM)
    system, right = pl.pallas_call(
        functools.partial(build_kernel, toks),
        out_shape=(
            jax.ShapeDtypeStruct((SIDE, SIDE, 2, 2, 2 * part, keep), F32),
            jax.ShapeDtypeStruct((share, width), F32),
        ),
        in_specs=[pl.BlockSpec(memory_space=pl.ANY), vmem, vmem],
        out_specs=(pl.BlockSpec(memory_space=pl.ANY), vmem),
        scratch_shapes=[
            pltpu.VMEM((2 * SIDE, SIDE, half, width), BF16),
            pltpu.VMEM((cols + band, 2 * half), BF16),
            pltpu.VMEM((cols + band, width), F32),
            pltpu.VMEM((cols, width), BF16),
            pltpu.VMEM((1, width + 128), F32),
            pltpu.VMEM((toks, 1, width + 128), F32),
            pltpu.VMEM((2, 4, part, keep), F32),
            pltpu.VMEM((4, part, keep), F32),
            pltpu.VMEM((4, part, keep), F32),
            pltpu.VMEM((3, part, keep), F32),
            pltpu.VMEM((part, keep), F32),
            pltpu.VMEM((4, share, width), F32),
            pltpu.VMEM((4, share, width), F32),
            pltpu.VMEM((2, share // 2, width), F32),
            pltpu.VMEM((2, share, width), F32),
            pltpu.SemaphoreType.DMA((copies,)),
            pltpu.SemaphoreType.DMA((copies,)),
            pltpu.SemaphoreType.DMA((2,)),
            pltpu.SemaphoreType.DMA((toks,)),
            pltpu.SemaphoreType.DMA((toks,)),
        ],
        compiler_params=pltpu.CompilerParams(collective_id=0, has_side_effects=True, vmem_limit_bytes=60 << 20),
        name="build",
    )(masked, ids, weight)
    return system.reshape(width, keep), right


def spread_kernel(a_ref, out, send, recv, own):
    e = lax.axis_index("expert")
    y, c = e // 2, e % 2
    share = a_ref.shape[0]
    rc = functools.partial(remote, (send, recv))

    def chip(yy):
        return {"expert": yy * 2 + c}

    partner = {"expert": e + 1 - 2 * c}
    up, down, across = near(y, 1), near(y, -1), near(y, 2)
    meet([partner, chip(up), chip(down)])
    half = share // 2
    first = [rc(0, a_ref, out.at[y, c], chip(up)), rc(1, a_ref, out.at[y, c], chip(down))]
    pairs = [rc(2, a_ref, out.at[y, c], partner)]
    for copy in first + pairs:
        copy.start()
    keep = pltpu.make_async_copy(a_ref, out.at[y, c], own.at[0])
    keep.start()
    lower, upper = out.at[down, c, pl.ds(0, half)], out.at[up, c, pl.ds(half, half)]
    onward = [rc(3, lower, lower, chip(up)), rc(4, upper, upper, chip(down))]
    for k, (got, copy, at) in enumerate(zip(first, onward, (down, up))):
        got.wait_recv()
        copy.start()
        forward = rc(5 + k, out.at[at, c], out.at[at, c], partner)
        forward.start()
        pairs.append(forward)
    for k, copy in enumerate(onward):
        copy.wait_recv()
        part = out.at[across, c, pl.ds(half * k, half)]
        forward = rc(7 + k, part, part, partner)
        forward.start()
        pairs.append(forward)
    keep.wait()
    for copy in pairs:
        copy.wait_recv()
    for copy in first + onward + pairs:
        copy.wait_send()


def spread(answer):
    share, width = answer.shape
    out = pl.pallas_call(
        spread_kernel,
        out_shape=jax.ShapeDtypeStruct((4, 2, share, width), F32),
        in_specs=[pl.BlockSpec(memory_space=pltpu.VMEM)],
        out_specs=pl.BlockSpec(memory_space=pl.ANY),
        scratch_shapes=[pltpu.SemaphoreType.DMA((9,)), pltpu.SemaphoreType.DMA((9,)), pltpu.SemaphoreType.DMA((1,))],
        compiler_params=pltpu.CompilerParams(collective_id=1, has_side_effects=True),
        name="spread",
    )(answer)
    return out.reshape(8 * share, width)


def solve_kernel(width, cols, t_hbm, b_ref, x_ref, stage, full, sh, sm, sl, dvec, dinv, stack, r, ri, p, d, q, rz, goal, nn, xx, sems):
    blk = width // sems.shape[0]
    loads = [
        pltpu.make_async_copy(t_hbm.at[pl.ds(i * blk, blk)], stage.at[pl.ds(i * blk, blk)], sems.at[i])
        for i in range(width // blk)
    ]
    for load in loads:
        load.start()
    band = 128
    bands = width // band
    eye = lax.broadcasted_iota(jnp.int32, (band, band), 0) == lax.broadcasted_iota(jnp.int32, (band, band), 1)

    def block(i):
        return pl.ds(pl.multiple_of(i * band, band), band)

    for i, load in enumerate(loads):
        load.wait()

        def unfold(t, c):
            for o in range(bands // 2 + 1):
                j = (t + o) % bands
                tile = stage[block(t), o * band : (o + 1) * band]
                full[block(t), block(j)] = tile
                sh[block(t), block(j)] = tile.astype(BF16)
                if o == 0:
                    dvec[:, block(t)] = jnp.sum(jnp.where(eye, tile, 0.0), axis=0, keepdims=True)
                elif o < bands // 2:
                    turned = tile.T
                    full[block(j), block(t)] = turned
                    sh[block(j), block(t)] = turned.astype(BF16)
            return c

        lax.fori_loop(i * blk // band, (i + 1) * blk // band, unfold, 0)
    dinv[...] = 1.0 / dvec[...]

    parts = cols // ROWS

    def at(i, which=0):
        return slice(which * cols + i * ROWS, which * cols + (i + 1) * ROWS)

    def lanes(v):
        return jnp.broadcast_to(v, (ROWS, 128))

    def total(v):
        return jnp.sum(v, axis=1, keepdims=True)

    def halves(i, v):
        high = v.astype(BF16)
        low = (v - high.astype(F32)).astype(BF16)
        stack[at(i), :] = high
        stack[at(i, 1), :] = low
        return high.astype(F32) + low.astype(F32)

    def dot(rows, piece):
        return jnp.dot(stack[:rows, :], piece[...], preferred_element_type=F32)

    for i in range(parts):
        b = b_ref[at(i), :]
        x_ref[at(i), :] = jnp.zeros_like(b)
        r[at(i), :] = b
        nn[at(i), :] = lanes(total(b * b * dinv[...]))
        xx[at(i), :] = jnp.zeros((ROWS, 128), F32)

    def outer(carry):
        k, _ = carry
        for i in range(parts):
            v = r[at(i), :]
            ri[at(i), :] = v
            p[at(i), :] = halves(i, v * dinv[...])
            d[at(i), :] = jnp.zeros_like(v)
            rz[at(i), :] = nn[at(i), :]
            goal[at(i), :] = jnp.maximum(nn[at(i), :] * (INNER_TOL * INNER_TOL), xx[at(i), :] * (0.25 * OUTER_TOL * OUTER_TOL))

        def inner(carry):
            it, _ = carry
            wide = dot(2 * cols, sh)
            q[...] = 0.9 * (wide[:cols] + wide[cols:])

            @pl.when(k >= 2)
            def _():
                q[...] += 0.9 * dot(cols, sm)

            worst = jnp.float32(-1.0)
            for i in range(parts):
                v = p[at(i), :]
                w = q[at(i), :] + 0.1 * dvec[...] * v
                old = rz[at(i), :1]
                pq = total(v * w)
                alpha = jnp.where(pq > 0, old / jnp.where(pq > 0, pq, 1.0), 0.0)
                d[at(i), :] += alpha * v
                res = ri[at(i), :] - alpha * w
                ri[at(i), :] = res
                z = res * dinv[...]
                new = total(res * z)
                beta = jnp.where(old > 0, new / jnp.where(old > 0, old, 1.0), 0.0)
                p[at(i), :] = halves(i, z + beta * v)
                rz[at(i), :] = lanes(new)
                worst = jnp.maximum(worst, jnp.max(new - goal[at(i), :1]))
            return it + 1, worst

        cap = jnp.where(k < 2, 64, 4000)
        lax.while_loop(lambda c: jnp.logical_and(c[0] < cap, c[1] > 0), inner, (jnp.int32(0), jnp.float32(1.0)))

        @pl.when(k == 0)
        def _():
            def rest(j, c):
                at = pl.ds(pl.multiple_of(j * 32, 32), 32)
                left = full[at, :] - sh[at, :].astype(F32)
                mid = left.astype(BF16)
                sm[at, :] = mid
                sl[at, :] = (left - mid.astype(F32)).astype(BF16)
                return c

            lax.fori_loop(0, width // 32, rest, 0)

        for i in range(parts):
            halves(i, d[at(i), :])
            d[at(i), :] += x_ref[at(i), :]

        @pl.when(k < 2)
        def _():
            wide = dot(2 * cols, sm)
            q[...] = ri[...] - 0.9 * (wide[:cols] + wide[cols:])

            @pl.when(k == 1)
            def _():
                for i in range(parts):
                    stack[at(i), :] = d[at(i), :].astype(BF16)
                q[...] -= 0.9 * dot(cols, sl)

        @pl.when(k >= 2)
        def _():
            for i in range(parts):
                v = d[at(i), :]
                stack[at(i, 2), :] = (v - halves(i, v)).astype(BF16)
                q[at(i), :] = b_ref[at(i), :] - 0.1 * dvec[...] * v
            wide = dot(3 * cols, sh)
            q[...] -= 0.9 * (wide[:cols] + wide[cols : 2 * cols] + wide[2 * cols :])
            wide = dot(2 * cols, sm)
            q[...] -= 0.9 * (wide[:cols] + wide[cols:])
            q[...] -= 0.9 * dot(cols, sl)

        worst = jnp.float32(-1.0)
        for i in range(parts):
            new = q[at(i), :]
            size = total(new * new * dinv[...])
            better = size < nn[at(i), :1]
            x = jnp.where(better, d[at(i), :], x_ref[at(i), :])
            x_ref[at(i), :] = x
            r[at(i), :] = jnp.where(better, new, r[at(i), :])
            kept = jnp.where(better, size, nn[at(i), :1])
            nn[at(i), :] = lanes(kept)
            norm = total(x * x * dvec[...])
            xx[at(i), :] = lanes(norm)
            worst = jnp.maximum(worst, jnp.max(kept - (OUTER_TOL * OUTER_TOL) * norm))
        return k + 1, worst

    def more(carry):
        return jnp.logical_or(carry[0] < 2, jnp.logical_and(carry[0] < 20, carry[1] > 0))

    lax.while_loop(more, outer, (jnp.int32(0), jnp.float32(1.0)))


def solve(system, right):
    width, keep = system.shape
    cols = right.shape[0]
    vec = pltpu.VMEM((cols, width), F32)
    col = pltpu.VMEM((cols, 128), F32)
    piece = pltpu.VMEM((width, width), BF16)
    row = pltpu.VMEM((1, width), F32)
    return pl.pallas_call(
        functools.partial(solve_kernel, width, cols),
        out_shape=jax.ShapeDtypeStruct((cols, width), F32),
        in_specs=[pl.BlockSpec(memory_space=pl.ANY), pl.BlockSpec(memory_space=pltpu.VMEM)],
        out_specs=pl.BlockSpec(memory_space=pltpu.VMEM),
        scratch_shapes=[
            pltpu.VMEM((width, keep), F32),
            pltpu.VMEM((width, width), F32),
            piece, piece, piece,
            row, row,
            pltpu.VMEM((3 * cols, width), BF16),
            vec, vec, vec, vec, vec,
            col, col, col, col,
            pltpu.SemaphoreType.DMA((8,)),
        ],
        compiler_params=pltpu.CompilerParams(vmem_limit_bytes=60 << 20),
        name="solve",
    )(system, right)


def local(hidden, token_ids, weights):
    live = token_ids[0] != 128004
    masked = jnp.where(live[:, None], hidden[0], 0)
    system, right = build(masked, token_ids.reshape(-1, 128), weights[0], lax.axis_size("tok"))
    return spread(solve(system, right)).T


def solution(mesh):
    return jax.shard_map(
        local,
        mesh=mesh,
        in_specs=(P("expert", "tok", None), P("expert", "tok"), P("expert", None, "tok")),
        out_specs=P(None, "tok"),
        check_vma=False,
    )
```

profile of v0, /device:TPU:1, one launch (start us, length us, event | category | flops | bytes accessed | tf_op | source)
XLA Modules:
  0.0 376.8 jit_solution(1252865632417557675)
XLA Ops:
  0.0 0.7 compare_reduce_fusion
  0.7 2.3 bitcast_select_fusion.x_hbm
  3.0 152.1 %build.1 = (f32[4,4,2,2,32,1152]{5,4,3,2,1,0:T(8,128)}, f32[64,2048]{1,0:T(8,128)}) custom-call(bf16[256,2048]{1,0:T(8,128)(2,1)} %bitcast_select_fusion.x_hbm, s32[2,128]{1,0:T(2,128)} %bitcast.10, bf16[2048,512]{1,0:T(8,128)(2,1)} %bitcast.9), custom_call_target="tpu_custom_call" | custom-call | tf_op jit(solution)/shard_map/build/pallas_call | solution.py:345
  155.1 183.2 %solve.1.a_ref = f32[64,2048]{1,0:T(8,128)} custom-call(f32[2048,1152]{1,0:T(8,128)} %bitcast.8, f32[64,2048]{1,0:T(8,128)} %get-tuple-element.8.b_ref), custom_call_target="tpu_custom_call" | custom-call | tf_op jit(solution)/shard_map/solve/pallas_call | solution.py:605
  338.4 33.1 %spread.1 = f32[4,2,64,2048]{3,2,1,0:T(8,128)} custom-call(f32[64,2048]{1,0:T(8,128)} %solve.1.a_ref), custom_call_target="tpu_custom_call" | custom-call | tf_op jit(solution)/shard_map/spread/pallas_call | solution.py:423
  371.5 5.3 %copy.4 = f32[512,2048]{0,1:T(8,128)} copy(f32[512,2048]{1,0:T(8,128)} %bitcast.7) | data formatting | bytes 8388608 | tf_op jit(solution)/shard_map/reshape | solution.py:432
where the time goes:
time: 384 us; the launch traced here: 377 us
  Pallas kernels  368 us (96%)
  local copies, waits for them, and re-layouts  5.35 us (1%)
    pallas_call x1, Pallas kernels, solve(): pl.pallas_call(functools.partial(solve_kernel, width, cols), out_shape=ja...  183 us
    pallas_call x1, Pallas kernels, build(): pl.pallas_call(functools.partial(build_kernel, toks), out_shape=(jax.Shap...  152 us
    pallas_call x1, Pallas kernels, spread(): pl.pallas_call(spread_kernel, out_shape=jax.ShapeDtypeStruct((4, 2, share...  33.1 us

commit v1 on v0

--- a/solution.py
+++ b/solution.py
@@ -10,8 +10,8 @@
 F32, BF16 = jnp.float32, jnp.bfloat16
 MESH = pl.DeviceIdType.MESH
 SIDE = 4
-INNER_TOL = 4e-3
-OUTER_TOL = 2e-5
+INNER_TOL = 8e-3
+OUTER_TOL = 5e-5
 ROWS = 16
 
 
@@ -34,7 +34,7 @@
     pl.semaphore_wait(barrier, len(devices))
 
 
-def build_kernel(toks, x_hbm, ids_ref, w_ref, s, b_ref, X, cat, acc, wt, stat, stats, gr, pg, hg, rg, sg, pt, ht, far, close,
+def build_kernel(toks, x_hbm, ids_ref, w_ref, s, b_ref, raw, X, cat, acc, wt, stat, stats, gr, pg, hg, rg, sg, pt, ht, far, close,
                  send, recv, own, stat_send, stat_recv):
     e, t = lax.axis_index("expert"), lax.axis_index("tok")
     y, c = e // 2, e % 2
@@ -55,11 +55,16 @@
 
     partner = {"expert": e + 1 - 2 * c}
     up, down, across = near(y, 1), near(y, -1), near(y, 2)
+    loads = [pltpu.make_async_copy(x_hbm.at[pl.ds(k * half, half)], raw.at[k], own.at[k]) for k in range(2)]
+    for load in loads:
+        load.start()
+    eye = lax.broadcasted_iota(jnp.int32, (half, half), 0) == lax.broadcasted_iota(jnp.int32, (half, half), 1)
+    alive = [
+        jnp.sum(jnp.where(eye, jnp.where(ids_ref[k : k + 1, :] != 128004, 1.0, 0.0), 0.0), axis=1, keepdims=True)
+        for k in range(2)
+    ]
     meet([{"tok": (t + k) % toks} for k in range(1, toks)] + [partner, chip(up), chip(down), chip(across)])
     mine = (X.at[z, x], X.at[SIDE + x, z])
-    loads = [pltpu.make_async_copy(x_hbm.at[pl.ds(k * half, half)], mine[k], own.at[k]) for k in range(2)]
-    for load in loads:
-        load.start()
 
     def stage(block, part, to, here):
         above, below = near(here, 1), near(here, -1)
@@ -73,11 +78,12 @@
     b_first, b_onward = stage(
         lambda i: X.at[SIDE + x, i], lambda i, h: X.at[SIDE + x, i, pl.ds(h * quarter, quarter)], lambda i: tok(i, x), z)
 
-    loads[0].wait()
-    for copy in a_first:
-        copy.start()
-    loads[1].wait()
-    for copy in b_first:
+    for k in range(2):
+        loads[k].wait()
+        for i in range(0, half, 2 * ROWS):
+            keep = alive[k][i : i + 2 * ROWS] > 0
+            mine[k][i : i + 2 * ROWS, :] = jnp.where(keep, raw[k, i : i + 2 * ROWS, :].astype(F32), 0.0).astype(BF16)
+    for copy in a_first + b_first:
         copy.start()
 
     def clear(i, k):
@@ -270,6 +276,10 @@
 
     finish(c)
 
+    for got, copy in zip(a_first_g + b_first_g, a_onward_g + b_onward_g):
+        got.wait_recv()
+        copy.start()
+
     for k in range(4):
         swap_t[k].wait_recv()
         ht[k] = acc[rows_of(k, c), :] + pt[k]
@@ -281,9 +291,6 @@
     for copy in first_t:
         copy.start()
 
-    for got, copy in zip(a_first_g + b_first_g, a_onward_g + b_onward_g):
-        got.wait_recv()
-        copy.start()
     for copy in a_onward_g + b_onward_g:
         copy.wait_recv()
 
@@ -333,8 +340,8 @@
     lax.fori_loop(1, toks, lambda k, v: (share(k).wait_send(), v)[1], 0)
 
 
-def build(masked, ids, weight, toks):
-    count, width = masked.shape
+def build(tokens, ids, weight, toks):
+    count, width = tokens.shape
     cols = weight.shape[1]
     band = width // toks
     half = count // 2
@@ -351,6 +358,7 @@
         in_specs=[pl.BlockSpec(memory_space=pl.ANY), vmem, vmem],
         out_specs=(pl.BlockSpec(memory_space=pl.ANY), vmem),
         scratch_shapes=[
+            pltpu.VMEM((2, half, width), BF16),
             pltpu.VMEM((2 * SIDE, SIDE, half, width), BF16),
             pltpu.VMEM((cols + band, 2 * half), BF16),
             pltpu.VMEM((cols + band, width), F32),
@@ -374,7 +382,7 @@
         ],
         compiler_params=pltpu.CompilerParams(collective_id=0, has_side_effects=True, vmem_limit_bytes=60 << 20),
         name="build",
-    )(masked, ids, weight)
+    )(tokens, ids, weight)
     return system.reshape(width, keep), right
 
 
@@ -391,30 +399,43 @@
     up, down, across = near(y, 1), near(y, -1), near(y, 2)
     meet([partner, chip(up), chip(down)])
     half = share // 2
-    first = [rc(0, a_ref, out.at[y, c], chip(up)), rc(1, a_ref, out.at[y, c], chip(down))]
-    pairs = [rc(2, a_ref, out.at[y, c], partner)]
-    for copy in first + pairs:
-        copy.start()
+
+    def part(at, h):
+        return out.at[at, c, pl.ds(half * h, half)]
+
+    mine = [a_ref.at[pl.ds(half * h, half)] for h in range(2)]
+    to_up = [rc(h, mine[h], part(y, h), chip(up)) for h in range(2)]
+    to_down = [rc(2 + h, mine[h], part(y, h), chip(down)) for h in range(2)]
+    onward = [rc(4, part(down, 0), part(down, 0), chip(up)), rc(5, part(up, 1), part(up, 1), chip(down))]
+    pairs = []
+
+    def hand(source, target):
+        copy = rc(6 + len(pairs), source, target, partner)
+        copy.start()
+        pairs.append(copy)
+
+    for copy in (to_up[0], to_down[1], to_up[1], to_down[0]):
+        copy.start()
+    hand(a_ref, out.at[y, c])
     keep = pltpu.make_async_copy(a_ref, out.at[y, c], own.at[0])
     keep.start()
-    lower, upper = out.at[down, c, pl.ds(0, half)], out.at[up, c, pl.ds(half, half)]
-    onward = [rc(3, lower, lower, chip(up)), rc(4, upper, upper, chip(down))]
-    for k, (got, copy, at) in enumerate(zip(first, onward, (down, up))):
-        got.wait_recv()
-        copy.start()
-        forward = rc(5 + k, out.at[at, c], out.at[at, c], partner)
-        forward.start()
-        pairs.append(forward)
-    for k, copy in enumerate(onward):
-        copy.wait_recv()
-        part = out.at[across, c, pl.ds(half * k, half)]
-        forward = rc(7 + k, part, part, partner)
-        forward.start()
-        pairs.append(forward)
+    to_up[0].wait_recv()
+    onward[0].start()
+    to_down[1].wait_recv()
+    onward[1].start()
+    hand(part(down, 0), part(down, 0))
+    hand(part(up, 1), part(up, 1))
+    to_up[1].wait_recv()
+    hand(part(down, 1), part(down, 1))
+    to_down[0].wait_recv()
+    hand(part(up, 0), part(up, 0))
+    for h in range(2):
+        onward[h].wait_recv()
+        hand(part(across, h), part(across, h))
     keep.wait()
     for copy in pairs:
         copy.wait_recv()
-    for copy in first + onward + pairs:
+    for copy in to_up + to_down + onward + pairs:
         copy.wait_send()
 
 
@@ -425,7 +446,7 @@
         out_shape=jax.ShapeDtypeStruct((4, 2, share, width), F32),
         in_specs=[pl.BlockSpec(memory_space=pltpu.VMEM)],
         out_specs=pl.BlockSpec(memory_space=pl.ANY),
-        scratch_shapes=[pltpu.SemaphoreType.DMA((9,)), pltpu.SemaphoreType.DMA((9,)), pltpu.SemaphoreType.DMA((1,))],
+        scratch_shapes=[pltpu.SemaphoreType.DMA((13,)), pltpu.SemaphoreType.DMA((13,)), pltpu.SemaphoreType.DMA((1,))],
         compiler_params=pltpu.CompilerParams(collective_id=1, has_side_effects=True),
         name="spread",
     )(answer)
@@ -514,22 +535,27 @@
             def _():
                 q[...] += 0.9 * dot(cols, sm)
 
-            worst = jnp.float32(-1.0)
-            for i in range(parts):
+            each = range(parts)
+            pq = []
+            for i in each:
                 v = p[at(i), :]
                 w = q[at(i), :] + 0.1 * dvec[...] * v
+                q[at(i), :] = w
+                pq.append(total(v * w))
+            alpha = [jnp.where(pq[i] > 0, rz[at(i), :1] / jnp.where(pq[i] > 0, pq[i], 1.0), 0.0) for i in each]
+            new = []
+            for i in each:
+                d[at(i), :] += alpha[i] * p[at(i), :]
+                res = ri[at(i), :] - alpha[i] * q[at(i), :]
+                ri[at(i), :] = res
+                new.append(total(res * res * dinv[...]))
+            worst = jnp.float32(-1.0)
+            for i in each:
                 old = rz[at(i), :1]
-                pq = total(v * w)
-                alpha = jnp.where(pq > 0, old / jnp.where(pq > 0, pq, 1.0), 0.0)
-                d[at(i), :] += alpha * v
-                res = ri[at(i), :] - alpha * w
-                ri[at(i), :] = res
-                z = res * dinv[...]
-                new = total(res * z)
-                beta = jnp.where(old > 0, new / jnp.where(old > 0, old, 1.0), 0.0)
-                p[at(i), :] = halves(i, z + beta * v)
-                rz[at(i), :] = lanes(new)
-                worst = jnp.maximum(worst, jnp.max(new - goal[at(i), :1]))
+                beta = jnp.where(old > 0, new[i] / jnp.where(old > 0, old, 1.0), 0.0)
+                p[at(i), :] = halves(i, ri[at(i), :] * dinv[...] + beta * p[at(i), :])
+                rz[at(i), :] = lanes(new[i])
+                worst = jnp.maximum(worst, jnp.max(new[i] - goal[at(i), :1]))
             return it + 1, worst
 
         cap = jnp.where(k < 2, 64, 4000)
@@ -539,10 +565,16 @@
         def _():
             def rest(j, c):
                 at = pl.ds(pl.multiple_of(j * 32, 32), 32)
-                left = full[at, :] - sh[at, :].astype(F32)
-                mid = left.astype(BF16)
-                sm[at, :] = mid
-                sl[at, :] = (left - mid.astype(F32)).astype(BF16)
+                sm[at, :] = (full[at, :] - sh[at, :].astype(F32)).astype(BF16)
+                return c
+
+            lax.fori_loop(0, width // 32, rest, 0)
+
+        @pl.when(k == 2)
+        def _():
+            def rest(j, c):
+                at = pl.ds(pl.multiple_of(j * 32, 32), 32)
+                sl[at, :] = (full[at, :] - sh[at, :].astype(F32) - sm[at, :].astype(F32)).astype(BF16)
                 return c
 
             lax.fori_loop(0, width // 32, rest, 0)
@@ -555,12 +587,6 @@
         def _():
             wide = dot(2 * cols, sm)
             q[...] = ri[...] - 0.9 * (wide[:cols] + wide[cols:])
-
-            @pl.when(k == 1)
-            def _():
-                for i in range(parts):
-                    stack[at(i), :] = d[at(i), :].astype(BF16)
-                q[...] -= 0.9 * dot(cols, sl)
 
         @pl.when(k >= 2)
         def _():
@@ -590,7 +616,7 @@
         return k + 1, worst
 
     def more(carry):
-        return jnp.logical_or(carry[0] < 2, jnp.logical_and(carry[0] < 20, carry[1] > 0))
+        return jnp.logical_and(carry[0] < 20, carry[1] > 0)
 
     lax.while_loop(more, outer, (jnp.int32(0), jnp.float32(1.0)))
 
@@ -623,9 +649,7 @@
 
 
 def local(hidden, token_ids, weights):
-    live = token_ids[0] != 128004
-    masked = jnp.where(live[:, None], hidden[0], 0)
-    system, right = build(masked, token_ids.reshape(-1, 128), weights[0], lax.axis_size("tok"))
+    system, right = build(hidden[0], token_ids.reshape(-1, 128), weights[0], lax.axis_size("tok"))
     return spread(solve(system, right)).T
 
 

time: 384 us -> 355 us (0.924); the launches traced: 377 us -> 356 us
  Pallas kernels: 368 us -> 351 us
    pallas_call x1, Pallas kernels: 183 us -> 165 us  [solve(): pl.pallas_call(functools.partial(solve_kernel, width, cols), out_shape=ja...]
where the time goes in v1:
time: 355 us; the launch traced here: 356 us
  Pallas kernels  351 us (99%)
  local copies, waits for them, and re-layouts  5.35 us (2%)
    pallas_call x1, Pallas kernels, solve(): pl.pallas_call(functools.partial(solve_kernel, width, cols), out_shape=ja...  165 us
    pallas_call x1, Pallas kernels, build(): pl.pallas_call(functools.partial(build_kernel, toks), out_shape=(jax.Shap...  151 us
    pallas_call x1, Pallas kernels, spread(): pl.pallas_call(spread_kernel, out_shape=jax.ShapeDtypeStruct((4, 2, share...  33.9 us

profile of v1, /device:TPU:1, one launch (start us, length us, event | category | flops | bytes accessed | tf_op | source)
XLA Modules:
  0.0 356.1 jit_solution(17285455220130345967)
XLA Ops:
  0.0 151.5 %build.1 = (f32[4,4,2,2,32,1152]{5,4,3,2,1,0:T(8,128)}, f32[64,2048]{1,0:T(8,128)}) custom-call(bf16[256,2048]{1,0:T(8,128)(2,1)} %bitcast.9, s32[2,128]{1,0:T(2,128)} %bitcast.10, bf16[2048,512]{1,0:T(8,128)(2,1)} %bitcast.8), custom_call_target="tpu_custom_call" | custom-call | tf_op jit(solution)/shard_map/build/pallas_call | solution.py:352
  151.5 165.3 %solve.1.a_ref = f32[64,2048]{1,0:T(8,128)} custom-call(f32[2048,1152]{1,0:T(8,128)} %bitcast.7, f32[64,2048]{1,0:T(8,128)} %get-tuple-element.8.b_ref), custom_call_target="tpu_custom_call" | custom-call | tf_op jit(solution)/shard_map/solve/pallas_call | solution.py:631
  316.8 33.9 %spread.1 = f32[4,2,64,2048]{3,2,1,0:T(8,128)} custom-call(f32[64,2048]{1,0:T(8,128)} %solve.1.a_ref), custom_call_target="tpu_custom_call" | custom-call | tf_op jit(solution)/shard_map/spread/pallas_call | solution.py:444
  350.7 5.3 %copy.4 = f32[512,2048]{0,1:T(8,128)} copy(f32[512,2048]{1,0:T(8,128)} %bitcast.6) | data formatting | bytes 8388608 | tf_op jit(solution)/shard_map/reshape | solution.py:453

commit v2 on v1

--- a/solution.py
+++ b/solution.py
@@ -111,8 +111,28 @@
 
     lax.fori_loop(0, width // 256, turn, 0)
 
+    def group(pair_of, slot_of, to, here, inner):
+        above, below = near(here, 1), near(here, -1)
+        first, onward = [], []
+        for part in range(2):
+            h = pair_at(part, inner)
+            block = pair_of(here, h)
+            first.append([rc(block, block, to(above)), rc(block, block, to(below))])
+            lower, upper = slot_of(below, 2 * h), slot_of(above, 2 * h + 1)
+            onward.append([rc(lower, lower, to(above)), rc(upper, upper, to(below))])
+        return first, onward
+
+    def pair_at(part, inner):
+        return inner // 2 * (1 - part) + (1 - inner // 2) * part
+
+    a_near, a_far = group(lambda i, h: X.at[i, pl.ds(2 * h, 2)], lambda i, j: X.at[i, j], lambda i: tok(i, x), z, x)
+    b_near, b_far = group(
+        lambda i, h: X.at[SIDE + i, pl.ds(2 * h, 2)], lambda i, j: X.at[SIDE + i, j], lambda i: tok(z, i), x, z)
+
     for got, copy in zip(a_first + b_first, a_onward + b_onward):
         got.wait_recv()
+        copy.start()
+    for copy in a_near[0] + b_near[0]:
         copy.start()
 
     def share(k):
@@ -124,28 +144,16 @@
     for copy in a_onward + b_onward:
         copy.wait_recv()
 
-    def group(g_of, to, here):
-        above, below = near(here, 1), near(here, -1)
-        first, onward = [], []
-        for h in range(2):
-            part = X.at[g_of(here), pl.ds(2 * h, 2)]
-            first.append([rc(part, part, to(above)), rc(part, part, to(below))])
-            lower, upper = X.at[g_of(below), 2 * h], X.at[g_of(above), 2 * h + 1]
-            onward.append([rc(lower, lower, to(above)), rc(upper, upper, to(below))])
-        return first, onward
-
-    a_near, a_far = group(lambda i: i, lambda i: tok(i, x), z)
-    b_near, b_far = group(lambda i: SIDE + i, lambda i: tok(z, i), x)
-    for h in range(2):
-        for copy in a_near[h] + b_near[h]:
-            copy.start()
+    for copy in a_near[1] + b_near[1]:
+        copy.start()
 
     lax.fori_loop(1, toks, lambda k, v: (share(k).start(), v)[1], 0)
 
     pair = 2 * half
 
-    def blocks(kind, off, h):
+    def blocks(kind, off, part):
         here = z * (1 - kind) + x * kind
+        h = pair_at(part, x * (1 - kind) + z * kind)
         return X.at[kind * SIDE + (here + off) % SIDE, pl.ds(2 * h, 2)]
 
     def put_up(block):
@@ -276,8 +284,15 @@
 
     finish(c)
 
+    a_near_g, a_far_g = group(
+        lambda i, h: s.at[i, pl.ds(2 * h, 2), c, 0], lambda i, j: s.at[i, j, c, 0], lambda i: tok(i, x), z, x)
+    b_near_g, b_far_g = group(
+        lambda i, h: s.at[pl.ds(2 * h, 2), i, c, 1], lambda i, j: s.at[j, i, c, 1], lambda i: tok(z, i), x, z)
+
     for got, copy in zip(a_first_g + b_first_g, a_onward_g + b_onward_g):
         got.wait_recv()
+        copy.start()
+    for copy in a_near_g[0] + b_near_g[0]:
         copy.start()
 
     for k in range(4):
@@ -293,10 +308,7 @@
 
     for copy in a_onward_g + b_onward_g:
         copy.wait_recv()
-
-    a_near_g, a_far_g = stage(lambda i: s.at[i, :, c, 0], lambda i, h: s.at[i, pl.ds(2 * h, 2), c, 0], lambda i: tok(i, x), z)
-    b_near_g, b_far_g = stage(lambda i: s.at[:, i, c, 1], lambda i, h: s.at[pl.ds(2 * h, 2), i, c, 1], lambda i: tok(z, i), x)
-    for copy in a_near_g + b_near_g:
+    for copy in a_near_g[1] + b_near_g[1]:
         copy.start()
 
     def hand(block):
@@ -314,27 +326,34 @@
     for copy in second_t:
         copy.start()
 
-    for got, copy in zip(a_near_g + b_near_g, a_far_g + b_far_g):
-        got.wait_recv()
-        copy.start()
+    for part in range(2):
+        for got, copy in zip(a_near_g[part] + b_near_g[part], a_far_g[part] + b_far_g[part]):
+            got.wait_recv()
+            copy.start()
     hands += [hand(s.at[near(z, -1), :, c, 0]), hand(s.at[near(z, 1), :, c, 0])]
     hands += [hand(s.at[:, near(x, -1), c, 1]), hand(s.at[:, near(x, 1), c, 1])]
+
+    for part in range(2):
+        for copy in a_far_g[part] + b_far_g[part]:
+            copy.wait_recv()
+        hands += [
+            hand(s.at[near(z, 2), pl.ds(2 * pair_at(part, x), 2), c, 0]),
+            hand(s.at[pl.ds(2 * pair_at(part, z), 2), near(x, 2), c, 1]),
+        ]
 
     for copy in second_t:
         copy.wait_recv()
     b_ref[...] = ht[y] + close[0] + close[1]
 
-    for copy in a_far_g + b_far_g:
-        copy.wait_recv()
-    hands += [hand(s.at[near(z, 2), :, c, 0]), hand(s.at[:, near(x, 2), c, 1])]
     for copy in hands:
         copy.wait_recv()
 
     sent = a_first + b_first + a_onward + b_onward
     for h in range(2):
         sent += a_near[h] + b_near[h] + a_far[h] + b_far[h]
+        sent += a_near_g[h] + b_near_g[h] + a_far_g[h] + b_far_g[h]
     sent += [swap_g] + scatter + spread_g + swap_t + first_t + second_t
-    sent += a_first_g + b_first_g + a_onward_g + b_onward_g + a_near_g + b_near_g + a_far_g + b_far_g + hands
+    sent += a_first_g + b_first_g + a_onward_g + b_onward_g + hands
     for copy in sent:
         copy.wait_send()
     lax.fori_loop(1, toks, lambda k, v: (share(k).wait_send(), v)[1], 0)
@@ -347,7 +366,7 @@
     half = count // 2
     keep = (toks // 2 + 1) * band
     part, share = band // 8, cols // 8
-    copies = 67
+    copies = 80
     vmem = pl.BlockSpec(memory_space=pltpu.VMEM)
     system, right = pl.pallas_call(
         functools.partial(build_kernel, toks),

time: 355 us -> 348 us (0.980)
  Pallas kernels: 351 us -> 346 us
    pallas_call x1, Pallas kernels: 33.9 us -> 24.4 us  [spread(): pl.pallas_call(spread_kernel, out_shape=jax.ShapeDtypeStruct((4, 2, share...]
    pallas_call x1, Pallas kernels: 165 us -> 174 us  [solve(): pl.pallas_call(functools.partial(solve_kernel, width, cols), out_shape=ja...]
    pallas_call x1, Pallas kernels: 151 us -> 148 us  [build(): pl.pallas_call(functools.partial(build_kernel, toks), out_shape=(jax.Shap...]
where the time goes in v2:
time: 348 us; the launch traced here: 351 us
  Pallas kernels  346 us (99%)
  local copies, waits for them, and re-layouts  5.35 us (2%)
    pallas_call x1, Pallas kernels, solve(): pl.pallas_call(functools.partial(solve_kernel, width, cols), out_shape=ja...  174 us
    pallas_call x1, Pallas kernels, build(): pl.pallas_call(functools.partial(build_kernel, toks), out_shape=(jax.Shap...  148 us
    pallas_call x1, Pallas kernels, spread(): pl.pallas_call(spread_kernel, out_shape=jax.ShapeDtypeStruct((4, 2, share...  24.4 us

profile of v2, /device:TPU:1, one launch (start us, length us, event | category | flops | bytes accessed | tf_op | source)
XLA Modules:
  0.0 351.4 jit_solution(7003343845761563832)
XLA Ops:
  0.0 147.8 %build.1 = (f32[4,4,2,2,32,1152]{5,4,3,2,1,0:T(8,128)}, f32[64,2048]{1,0:T(8,128)}) custom-call(bf16[256,2048]{1,0:T(8,128)(2,1)} %bitcast.9, s32[2,128]{1,0:T(2,128)} %bitcast.10, bf16[2048,512]{1,0:T(8,128)(2,1)} %bitcast.8), custom_call_target="tpu_custom_call" | custom-call | tf_op jit(solution)/shard_map/build/pallas_call | solution.py:371
  147.8 173.9 %solve.1.a_ref = f32[64,2048]{1,0:T(8,128)} custom-call(f32[2048,1152]{1,0:T(8,128)} %bitcast.7, f32[64,2048]{1,0:T(8,128)} %get-tuple-element.8.b_ref), custom_call_target="tpu_custom_call" | custom-call | tf_op jit(solution)/shard_map/solve/pallas_call | solution.py:650
  321.7 24.4 %spread.1 = f32[4,2,64,2048]{3,2,1,0:T(8,128)} custom-call(f32[64,2048]{1,0:T(8,128)} %solve.1.a_ref), custom_call_target="tpu_custom_call" | custom-call | tf_op jit(solution)/shard_map/spread/pallas_call | solution.py:463
  346.1 5.3 %copy.4 = f32[512,2048]{0,1:T(8,128)} copy(f32[512,2048]{1,0:T(8,128)} %bitcast.6) | data formatting | bytes 8388608 | tf_op jit(solution)/shard_map/reshape | solution.py:472

commit v3 on v2

--- a/solution.py
+++ b/solution.py
@@ -34,7 +34,7 @@
     pl.semaphore_wait(barrier, len(devices))
 
 
-def build_kernel(toks, x_hbm, ids_ref, w_ref, s, b_ref, raw, X, cat, acc, wt, stat, stats, gr, pg, hg, rg, sg, pt, ht, far, close,
+def build_kernel(toks, x_hbm, ids_ref, w_hbm, s, b_ref, w_ref, raw, X, cat, acc, wt, stat, stats, gr, pg, hg, rg, sg, pt, ht, far, close,
                  send, recv, own, stat_send, stat_recv):
     e, t = lax.axis_index("expert"), lax.axis_index("tok")
     y, c = e // 2, e % 2
@@ -58,6 +58,8 @@
     loads = [pltpu.make_async_copy(x_hbm.at[pl.ds(k * half, half)], raw.at[k], own.at[k]) for k in range(2)]
     for load in loads:
         load.start()
+    weights = pltpu.make_async_copy(w_hbm, w_ref, own.at[2])
+    weights.start()
     eye = lax.broadcasted_iota(jnp.int32, (half, half), 0) == lax.broadcasted_iota(jnp.int32, (half, half), 1)
     alive = [
         jnp.sum(jnp.where(eye, jnp.where(ids_ref[k : k + 1, :] != 128004, 1.0, 0.0), 0.0), axis=1, keepdims=True)
@@ -103,6 +105,8 @@
 
     stat[:, :width] = lax.fori_loop(0, half // ROWS, square, jnp.zeros((1, width), F32))
     stat[:, width:] = jnp.broadcast_to(live, (1, 128))
+
+    weights.wait()
 
     def turn(i, k):
         at = pl.ds(pl.multiple_of(i * 256, 256), 256)
@@ -374,9 +378,10 @@
             jax.ShapeDtypeStruct((SIDE, SIDE, 2, 2, 2 * part, keep), F32),
             jax.ShapeDtypeStruct((share, width), F32),
         ),
-        in_specs=[pl.BlockSpec(memory_space=pl.ANY), vmem, vmem],
+        in_specs=[pl.BlockSpec(memory_space=pl.ANY), vmem, pl.BlockSpec(memory_space=pl.ANY)],
         out_specs=(pl.BlockSpec(memory_space=pl.ANY), vmem),
         scratch_shapes=[
+            pltpu.VMEM((width, cols), BF16),
             pltpu.VMEM((2, half, width), BF16),
             pltpu.VMEM((2 * SIDE, SIDE, half, width), BF16),
             pltpu.VMEM((cols + band, 2 * half), BF16),
@@ -395,7 +400,7 @@
             pltpu.VMEM((2, share, width), F32),
             pltpu.SemaphoreType.DMA((copies,)),
             pltpu.SemaphoreType.DMA((copies,)),
-            pltpu.SemaphoreType.DMA((2,)),
+            pltpu.SemaphoreType.DMA((3,)),
             pltpu.SemaphoreType.DMA((toks,)),
             pltpu.SemaphoreType.DMA((toks,)),
         ],
@@ -472,7 +477,7 @@
     return out.reshape(8 * share, width)
 
 
-def solve_kernel(width, cols, t_hbm, b_ref, x_ref, stage, full, sh, sm, sl, dvec, dinv, stack, r, ri, p, d, q, rz, goal, nn, xx, sems):
+def solve_kernel(width, cols, t_hbm, b_ref, x_ref, stage, sh, sm, sl, dvec, dinv, stack, r, ri, p, d, q, rz, goal, nn, xx, sems):
     blk = width // sems.shape[0]
     loads = [
         pltpu.make_async_copy(t_hbm.at[pl.ds(i * blk, blk)], stage.at[pl.ds(i * blk, blk)], sems.at[i])
@@ -487,6 +492,14 @@
     def block(i):
         return pl.ds(pl.multiple_of(i * band, band), band)
 
+    def pieces(row, column, tile):
+        high = tile.astype(BF16)
+        sh[row, column] = high
+        sm[row, column] = (tile - high.astype(F32)).astype(BF16)
+
+    def lowest(row, column, tile):
+        sl[row, column] = (tile - sh[row, column].astype(F32) - sm[row, column].astype(F32)).astype(BF16)
+
     for i, load in enumerate(loads):
         load.wait()
 
@@ -494,14 +507,11 @@
             for o in range(bands // 2 + 1):
                 j = (t + o) % bands
                 tile = stage[block(t), o * band : (o + 1) * band]
-                full[block(t), block(j)] = tile
-                sh[block(t), block(j)] = tile.astype(BF16)
+                pieces(block(t), block(j), tile)
                 if o == 0:
                     dvec[:, block(t)] = jnp.sum(jnp.where(eye, tile, 0.0), axis=0, keepdims=True)
                 elif o < bands // 2:
-                    turned = tile.T
-                    full[block(j), block(t)] = turned
-                    sh[block(j), block(t)] = turned.astype(BF16)
+                    pieces(block(j), block(t), tile.T)
             return c
 
         lax.fori_loop(i * blk // band, (i + 1) * blk // band, unfold, 0)
@@ -580,23 +590,18 @@
         cap = jnp.where(k < 2, 64, 4000)
         lax.while_loop(lambda c: jnp.logical_and(c[0] < cap, c[1] > 0), inner, (jnp.int32(0), jnp.float32(1.0)))
 
-        @pl.when(k == 0)
-        def _():
-            def rest(j, c):
-                at = pl.ds(pl.multiple_of(j * 32, 32), 32)
-                sm[at, :] = (full[at, :] - sh[at, :].astype(F32)).astype(BF16)
-                return c
-
-            lax.fori_loop(0, width // 32, rest, 0)
-
         @pl.when(k == 2)
         def _():
-            def rest(j, c):
-                at = pl.ds(pl.multiple_of(j * 32, 32), 32)
-                sl[at, :] = (full[at, :] - sh[at, :].astype(F32) - sm[at, :].astype(F32)).astype(BF16)
+            def unfold(t, c):
+                for o in range(bands // 2 + 1):
+                    j = (t + o) % bands
+                    tile = stage[block(t), o * band : (o + 1) * band]
+                    lowest(block(t), block(j), tile)
+                    if 0 < o < bands // 2:
+                        lowest(block(j), block(t), tile.T)
                 return c
 
-            lax.fori_loop(0, width // 32, rest, 0)
+            lax.fori_loop(0, bands, unfold, 0)
 
         for i in range(parts):
             halves(i, d[at(i), :])
@@ -654,7 +659,6 @@
         out_specs=pl.BlockSpec(memory_space=pltpu.VMEM),
         scratch_shapes=[
             pltpu.VMEM((width, keep), F32),
-            pltpu.VMEM((width, width), F32),
             piece, piece, piece,
             row, row,
             pltpu.VMEM((3 * cols, width), BF16),

time: 348 us -> 354 us (1.017); the launches traced: 351 us -> 353 us
    pallas_call x1, Pallas kernels: 24.4 us -> 37.9 us  [spread(): pl.pallas_call(spread_kernel, out_shape=jax.ShapeDtypeStruct((4, 2, share...]
    pallas_call x1, Pallas kernels: 174 us -> 163 us  [solve(): pl.pallas_call(functools.partial(solve_kernel, width, cols), out_shape=ja...]
where the time goes in v3:
time: 354 us; the launch traced here: 353 us
  Pallas kernels  348 us (98%)
  local copies, waits for them, and re-layouts  5.35 us (2%)
    pallas_call x1, Pallas kernels, solve(): pl.pallas_call(functools.partial(solve_kernel, width, cols), out_shape=ja...  163 us
    pallas_call x1, Pallas kernels, build(): pl.pallas_call(functools.partial(build_kernel, toks), out_shape=(jax.Shap...  147 us
    pallas_call x1, Pallas kernels, spread(): pl.pallas_call(spread_kernel, out_shape=jax.ShapeDtypeStruct((4, 2, share...  37.9 us

profile of v3, /device:TPU:1, one launch (start us, length us, event | category | flops | bytes accessed | tf_op | source)
XLA Modules:
  0.0 353.3 jit_solution(2545624318832915922)
XLA Ops:
  0.0 146.8 %build.1 = (f32[4,4,2,2,32,1152]{5,4,3,2,1,0:T(8,128)}, f32[64,2048]{1,0:T(8,128)}) custom-call(bf16[256,2048]{1,0:T(8,128)(2,1)} %bitcast.9, s32[2,128]{1,0:T(2,128)} %bitcast.10, bf16[2048,512]{1,0:T(8,128)(2,1)} %bitcast.8), custom_call_target="tpu_custom_call" | custom-call | tf_op jit(solution)/shard_map/build/pallas_call | solution.py:375
  146.9 163.2 %solve.1.a_ref = f32[64,2048]{1,0:T(8,128)} custom-call(f32[2048,1152]{1,0:T(8,128)} %bitcast.7, f32[64,2048]{1,0:T(8,128)} %get-tuple-element.8.b_ref), custom_call_target="tpu_custom_call" | custom-call | tf_op jit(solution)/shard_map/solve/pallas_call | solution.py:655
  310.0 37.9 %spread.1 = f32[4,2,64,2048]{3,2,1,0:T(8,128)} custom-call(f32[64,2048]{1,0:T(8,128)} %solve.1.a_ref), custom_call_target="tpu_custom_call" | custom-call | tf_op jit(solution)/shard_map/spread/pallas_call | solution.py:468
  348.0 5.3 %copy.4 = f32[512,2048]{0,1:T(8,128)} copy(f32[512,2048]{1,0:T(8,128)} %bitcast.6) | data formatting | bytes 8388608 | tf_op jit(solution)/shard_map/reshape | solution.py:477

commit v4 on v3

--- a/solution.py
+++ b/solution.py
@@ -233,11 +233,7 @@
     swap_g = rc(gr.at[1 - c], pg, partner)
     swap_g.start()
 
-    def finish_up(kind):
-        put_up(blocks(kind, 2, 1))
-        add(blocks(kind, 2, 1), 0, cols)
-
-    finish_up(0)
+    put_up(blocks(0, 2, 1))
 
     swap_g.wait_recv()
     for k in range(4):
@@ -246,7 +242,8 @@
     for copy in scatter:
         copy.start()
 
-    finish_up(1)
+    add(blocks(0, 2, 1), 0, cols)
+    put_up(blocks(1, 2, 1))
 
     for copy in scatter:
         copy.wait_recv()
@@ -254,10 +251,15 @@
     rows = s.at[z, x, c, y // 2, pl.ds((y % 2) * ROWS, ROWS)]
     keep = pltpu.make_async_copy(sg, rows, own.at[0])
     keep.start()
-    spread_g = [rc(sg, rows, chip(near(y, k))) for k in range(1, 4)]
+    def rows_at(yy, h):
+        return s.at[z, x, c, yy // 2, pl.ds((yy % 2) * ROWS + h * (ROWS // 2), ROWS // 2)]
+
+    spread_g = [rc(sg, rows, chip(up)), rc(sg, rows, chip(down))]
     for copy in spread_g:
         copy.start()
-
+    passed_g = [rc(rows_at(down, 0), rows_at(down, 0), chip(up)), rc(rows_at(up, 1), rows_at(up, 1), chip(down))]
+
+    add(blocks(1, 2, 1), 0, cols)
     share_rows = cols // 8
 
     def rows_of(yy, cc):
@@ -272,13 +274,16 @@
 
         lax.fori_loop(0, 4 * share_rows // ROWS, tile, 0)
 
+    for got, copy in zip(spread_g, passed_g):
+        got.wait_recv()
+        copy.start()
     finish(1 - c)
     swap_t = [rc(acc.at[rows_of(k, 1 - c)], pt.at[k], partner) for k in range(4)]
     for copy in swap_t:
         copy.start()
 
     keep.wait()
-    for copy in spread_g:
+    for copy in passed_g:
         copy.wait_recv()
 
     a_first_g, a_onward_g = stage(lambda i: s.at[z, i, c, 0], lambda i, h: s.at[z, i, c, 0, pl.ds(16 * h, 16)], lambda i: tok(z, i), x)
@@ -356,7 +361,7 @@
     for h in range(2):
         sent += a_near[h] + b_near[h] + a_far[h] + b_far[h]
         sent += a_near_g[h] + b_near_g[h] + a_far_g[h] + b_far_g[h]
-    sent += [swap_g] + scatter + spread_g + swap_t + first_t + second_t
+    sent += [swap_g] + scatter + spread_g + passed_g + swap_t + first_t + second_t
     sent += a_first_g + b_first_g + a_onward_g + b_onward_g + hands
     for copy in sent:
         copy.wait_send()

time: 354 us -> 355 us (level)
    pallas_call x1, Pallas kernels: 163 us -> 170 us  [solve(): pl.pallas_call(functools.partial(solve_kernel, width, cols), out_shape=ja...]
    pallas_call x1, Pallas kernels: 37.9 us -> 32 us  [spread(): pl.pallas_call(spread_kernel, out_shape=jax.ShapeDtypeStruct((4, 2, share...]
where the time goes in v4:
time: 355 us; the launch traced here: 356 us
  Pallas kernels  351 us (99%)
  local copies, waits for them, and re-layouts  5.35 us (2%)
    pallas_call x1, Pallas kernels, solve(): pl.pallas_call(functools.partial(solve_kernel, width, cols), out_shape=ja...  170 us
    pallas_call x1, Pallas kernels, build(): pl.pallas_call(functools.partial(build_kernel, toks), out_shape=(jax.Shap...  148 us
    pallas_call x1, Pallas kernels, spread(): pl.pallas_call(spread_kernel, out_shape=jax.ShapeDtypeStruct((4, 2, share...  32 us

profile of v4, /device:TPU:1, one launch (start us, length us, event | category | flops | bytes accessed | tf_op | source)
XLA Modules:
  0.0 356.0 jit_solution(15411816509751977055)
XLA Ops:
  0.0 148.1 %build.1 = (f32[4,4,2,2,32,1152]{5,4,3,2,1,0:T(8,128)}, f32[64,2048]{1,0:T(8,128)}) custom-call(bf16[256,2048]{1,0:T(8,128)(2,1)} %bitcast.9, s32[2,128]{1,0:T(2,128)} %bitcast.10, bf16[2048,512]{1,0:T(8,128)(2,1)} %bitcast.8), custom_call_target="tpu_custom_call" | custom-call | tf_op jit(solution)/shard_map/build/pallas_call | solution.py:380
  148.1 170.5 %solve.1.a_ref = f32[64,2048]{1,0:T(8,128)} custom-call(f32[2048,1152]{1,0:T(8,128)} %bitcast.7, f32[64,2048]{1,0:T(8,128)} %get-tuple-element.8.b_ref), custom_call_target="tpu_custom_call" | custom-call | tf_op jit(solution)/shard_map/solve/pallas_call | solution.py:660
  318.6 32.0 %spread.1 = f32[4,2,64,2048]{3,2,1,0:T(8,128)} custom-call(f32[64,2048]{1,0:T(8,128)} %solve.1.a_ref), custom_call_target="tpu_custom_call" | custom-call | tf_op jit(solution)/shard_map/spread/pallas_call | solution.py:473
  350.6 5.3 %copy.4 = f32[512,2048]{0,1:T(8,128)} copy(f32[512,2048]{1,0:T(8,128)} %bitcast.6) | data formatting | bytes 8388608 | tf_op jit(solution)/shard_map/reshape | solution.py:482

commit v5 on v3

--- a/solution.py
+++ b/solution.py
@@ -233,11 +233,7 @@
     swap_g = rc(gr.at[1 - c], pg, partner)
     swap_g.start()
 
-    def finish_up(kind):
-        put_up(blocks(kind, 2, 1))
-        add(blocks(kind, 2, 1), 0, cols)
-
-    finish_up(0)
+    put_up(blocks(0, 2, 1))
 
     swap_g.wait_recv()
     for k in range(4):
@@ -246,7 +242,8 @@
     for copy in scatter:
         copy.start()
 
-    finish_up(1)
+    add(blocks(0, 2, 1), 0, cols)
+    put_up(blocks(1, 2, 1))
 
     for copy in scatter:
         copy.wait_recv()
@@ -258,6 +255,7 @@
     for copy in spread_g:
         copy.start()
 
+    add(blocks(1, 2, 1), 0, cols)
     share_rows = cols // 8
 
     def rows_of(yy, cc):

time: 354 us -> 349 us (0.986)
    pallas_call x1, Pallas kernels: 37.9 us -> 27.2 us  [spread(): pl.pallas_call(spread_kernel, out_shape=jax.ShapeDtypeStruct((4, 2, share...]
    pallas_call x1, Pallas kernels: 163 us -> 172 us  [solve(): pl.pallas_call(functools.partial(solve_kernel, width, cols), out_shape=ja...]
where the time goes in v5:
time: 349 us; the launch traced here: 352 us
  Pallas kernels  346 us (99%)
  local copies, waits for them, and re-layouts  5.35 us (2%)
    pallas_call x1, Pallas kernels, solve(): pl.pallas_call(functools.partial(solve_kernel, width, cols), out_shape=ja...  172 us
    pallas_call x1, Pallas kernels, build(): pl.pallas_call(functools.partial(build_kernel, toks), out_shape=(jax.Shap...  147 us
    pallas_call x1, Pallas kernels, spread(): pl.pallas_call(spread_kernel, out_shape=jax.ShapeDtypeStruct((4, 2, share...  27.2 us

profile of v5, /device:TPU:1, one launch (start us, length us, event | category | flops | bytes accessed | tf_op | source)
XLA Modules:
  0.0 351.6 jit_solution(15657296112139673621)
XLA Ops:
  0.0 147.0 %build.1 = (f32[4,4,2,2,32,1152]{5,4,3,2,1,0:T(8,128)}, f32[64,2048]{1,0:T(8,128)}) custom-call(bf16[256,2048]{1,0:T(8,128)(2,1)} %bitcast.9, s32[2,128]{1,0:T(2,128)} %bitcast.10, bf16[2048,512]{1,0:T(8,128)(2,1)} %bitcast.8), custom_call_target="tpu_custom_call" | custom-call | tf_op jit(solution)/shard_map/build/pallas_call | solution.py:373
  147.0 172.0 %solve.1.a_ref = f32[64,2048]{1,0:T(8,128)} custom-call(f32[2048,1152]{1,0:T(8,128)} %bitcast.7, f32[64,2048]{1,0:T(8,128)} %get-tuple-element.8.b_ref), custom_call_target="tpu_custom_call" | custom-call | tf_op jit(solution)/shard_map/solve/pallas_call | solution.py:653
  319.1 27.2 %spread.1 = f32[4,2,64,2048]{3,2,1,0:T(8,128)} custom-call(f32[64,2048]{1,0:T(8,128)} %solve.1.a_ref), custom_call_target="tpu_custom_call" | custom-call | tf_op jit(solution)/shard_map/spread/pallas_call | solution.py:466
  346.3 5.3 %copy.4 = f32[512,2048]{0,1:T(8,128)} copy(f32[512,2048]{1,0:T(8,128)} %bitcast.6) | data formatting | bytes 8388608 | tf_op jit(solution)/shard_map/reshape | solution.py:475
